TPU v7x, 32 devices: a whole 2x2x4 slice. The times are simulated.
32 devices in a mesh: tm: 8 (over z, core), space: 4 (over y, x).
Axes of the slice: x: 2, y: 2, z: 4, core: 2. Of those that a mesh axis runs over, the one named last changes fastest.
Arguments:
- snapshots: bfloat16 [4096, 12288], P('tm', 'space')
- freq_ids: int32 [64], replicated, may hold values from 0 to 127
Outputs:
- gram: float32 [64, 2, 15, 15], P('tm')
All inputs are finite; a program needn't handle non-finite values.
Results may differ from a plain program's by a relative error of at most 0.00039.
Values may be sent and summed in bfloat16 or wider, within the bound.
No kernel may reach another device: no remote copies, remote signals or barrier semaphores. Data moves between devices by JAX's collectives and lax.ppermute only.
A program may use at most 64 MiB of HBM per device.

v0:
```python
import math
import jax
import jax.numpy as jnp
from jax import lax
from jax.sharding import PartitionSpec as P

NFFT = 512
F = 64


def shifted(block, axis, distance):
    devices = range(lax.axis_size(axis))
    route = [(i - distance, i) for i in devices if i - distance in devices]
    return lax.ppermute(block, axis, route)


def kernel_values(freqs, shifts, window_length):
    phase = freqs * shifts % window_length
    angle = 2.0 * math.pi / window_length * phase.astype(jnp.float32)
    window = 0.5 - 0.5 * jnp.cos(2.0 * math.pi / window_length * shifts.astype(jnp.float32))
    return (window * jnp.cos(angle), -window * jnp.sin(angle))


def local(snapshots, freq_ids):
    hop_len = NFFT // 2
    count_tm = lax.axis_size("tm")
    blocks = 2 * count_tm - 1
    device = lax.axis_index("tm")
    points = snapshots.shape[1]
    shifts = jnp.arange(NFFT, dtype=jnp.int32)
    real_part, imag_part = kernel_values(freq_ids[:, None], shifts[None, :], NFFT)
    table = jnp.stack([real_part, imag_part], axis=1).reshape(2 * F, NFFT).astype(jnp.bfloat16)
    leading = shifted(snapshots[:hop_len], "tm", -1)
    extended = jnp.concatenate([snapshots, leading], axis=0)
    pieces = []
    for slot in range(2):
        block = device * 2 + slot
        segment = extended[hop_len * slot : hop_len * slot + NFFT]
        result = jnp.dot(table, segment, preferred_element_type=jnp.float32)
        pieces.append(jnp.where(block < blocks, result, 0.0))
    owned = jnp.stack(pieces, axis=0).astype(jnp.bfloat16)
    owned = owned.reshape(2, F, 2, points)
    by_freq = lax.all_to_all(owned, "tm", split_axis=1, concat_axis=0, tiled=True)
    slots_all = by_freq.shape[0]
    resident_frequencies = by_freq.shape[1]
    stacked_snapshot_rows = jnp.transpose(by_freq, (1, 2, 0, 3)).reshape(
        resident_frequencies, 2 * slots_all, points
    )
    cross_product_terms = jnp.einsum(
        "tnf,tof->tno",
        stacked_snapshot_rows,
        stacked_snapshot_rows,
        preferred_element_type=jnp.float32,
    )
    gram_real_matrix = (
        cross_product_terms[:, :slots_all, :slots_all]
        + cross_product_terms[:, slots_all:, slots_all:]
    )
    imag_gram = (
        cross_product_terms[:, slots_all:, :slots_all]
        - cross_product_terms[:, :slots_all, slots_all:]
    )
    scale = 1.0 / (NFFT * points * lax.axis_size("space"))
    resident_gram_matrix = (
        jnp.stack([gram_real_matrix, imag_gram], axis=1)[:, :, :blocks, :blocks] * scale
    )
    return lax.psum(resident_gram_matrix, "space")


def solution(mesh):
    return jax.shard_map(
        local,
        mesh=mesh,
        in_specs=(P("tm", "space"), P()),
        out_specs=P("tm", None, None, None),
        check_vma=False,
    )
```

profile of v0, /device:TPU:0, one launch (start us, length us, event | category | flops | bytes accessed | tf_op | source)
XLA Modules:
  0.0 96.8 jit_solution(8468911311742353693)
XLA Ops:
  0.0 0.0 copy-start
  0.0 0.0 copy-start.2
  0.0 2.8 %slice.21 = bf16[256,3072]{1,0:T(8,128)(2,1)} slice(bf16[512,3072]{1,0:T(8,128)(2,1)} %param.2), slice={[0:256], [0:3072]} | slice | bytes 3145728 | tf_op jit(solution)/shard_map/slice | solution.py:33
  2.8 1.3 %collective-permute-start = (bf16[256,3072]{1,0:T(8,128)(2,1)}, bf16[256,3072]{1,0:T(8,128)(2,1)}, u32[]{:S(2)}, u32[]{:S(2)}) collective-permute-start(bf16[256,3072]{1,0:T(8,128)(2,1)} %slice.21), channel_id=1, source_target_pairs={{4,0},{8,4},{12,8},{16,12},{20,16},{24,20},{28,24},{5,1},{9,5},{13... | collective-permute-start | bytes 4718600 | tf_op jit(solution)/shard_map/ppermute | solution.py:14
  4.2 0.0 copy-done.2
  4.2 0.6 multiply_convert_fusion.1
  4.8 0.1 copy.13
  5.0 0.1 convert_element_type.35
  5.0 0.0 copy-done
  5.0 1.5 %fusion = bf16[128,3072]{1,0:T(8,128)(2,1)} fusion(bf16[128,512]{1,0:T(8,128)(2,1)S(1)} %convert_element_type.35, bf16[512,3072]{1,0:T(8,128)(2,1)S(1)} %copy-done, pred[]{:T(512)S(6)} %lt.12), kind=kOutput, calls=%fused_computation.2 | convolution fusion | flops 403439616 | bytes 4063233 | tf_op jit(solution)/shard_map/dot_general | solution.py:39
  6.5 2.8 %stack.25 = bf16[1,64,2,3072]{3,2,1,0:T(2,128)(2,1)} reshape(bf16[128,3072]{1,0:T(8,128)(2,1)} %fusion) | data formatting | bytes 1572864 | tf_op jit(solution)/shard_map/stack | solution.py:41
  9.4 0.0 collective-permute-done
  9.4 2.9 %fusion.1 = bf16[128,3072]{1,0:T(8,128)(2,1)} fusion(bf16[128,512]{1,0:T(8,128)(2,1)S(1)} %convert_element_type.35, bf16[256,3072]{1,0:T(8,128)(2,1)} %collective-permute-done, bf16[512,3072]{1,0:T(8,128)(2,1)S(1)} %copy-done, pred[]{:T(512)S(6)} %lt.14), kind=kOutput, calls=%fused_computation.3 | convolution fusion | flops 409731072 | bytes 5636097 | tf_op jit(solution)/shard_map/dot_general | solution.py:39
  12.3 0.0 copy-start.1
  12.3 2.2 %stack.26 = bf16[1,64,2,3072]{3,2,1,0:T(2,128)(2,1)S(1)} reshape(bf16[128,3072]{1,0:T(8,128)(2,1)} %fusion.1) | data formatting | bytes 1572864 | tf_op jit(solution)/shard_map/stack | solution.py:41
  14.5 0.0 copy-done.1
  14.5 2.1 %pad_maximum_fusion.2 = bf16[2,64,2,3072]{3,2,0,1:T(2,128)(2,1)S(1)} fusion(bf16[1,64,2,3072]{3,2,0,1:T(2,128)(2,1)S(1)} %bitcast.22, bf16[1,64,2,3072]{3,2,0,1:T(2,128)(2,1)S(1)} %bitcast.21), kind=kLoop, calls=%fused_computation.6 | loop fusion | flops 786432 | bytes 3145728 | tf_op jit(solution)/shard_map/stack | solution.py:41
  16.6 58.0 %all_to_all.18 = bf16[2,64,2,3072]{3,2,0,1:T(2,128)(2,1)S(1)} all-to-all(bf16[2,64,2,3072]{3,2,0,1:T(2,128)(2,1)S(1)} %pad_maximum_fusion.2), channel_id=1, replica_groups=mesh['tm'=8,'space'=4] {'tm'}, dimensions={1} | all-to-all | bytes 3145728 | tf_op jit(solution)/shard_map/all_to_all | solution.py:43
  74.6 1.7 %copy.16 = bf16[8,2,8,2,3072]{4,1,0,3,2:T(2,128)(2,1)S(1)} copy(bf16[8,2,8,2,3072]{4,3,1,2,0:T(2,128)(2,1)S(1)} %bitcast.20) | data formatting | bytes 3145728 | tf_op jit(solution)/shard_map/all_to_all | solution.py:43
  76.3 0.6 all_to_all.16
  76.9 0.5 fusion.14
  77.5 0.1 fusion.11
  77.6 18.4 %psum.7 = f32[8,2,15,15]{3,2,0,1:T(8,128)S(1)} all-reduce(f32[8,2,15,15]{3,2,0,1:T(8,128)S(1)} %fusion.6), channel_id=1, replica_groups=mesh['tm'=8,'space'=4] {'space'}, use_global_device_ids=true, to_apply=%region_0.1 | all-reduce | flops 3600 | bytes 28800 | tf_op jit(solution)/shard_map/psum | solution.py:67
  96.0 0.7 copy.17
  (3 shorter events, 0.1 us)
Async XLA Ops:
  0.0 5.0 %copy-start = (bf16[512,3072]{1,0:T(8,128)(2,1)S(1)}, bf16[512,3072]{1,0:T(8,128)(2,1)}, u32[]{:S(2)}) copy-start(bf16[512,3072]{1,0:T(8,128)(2,1)} %param.2) | copy-start | bytes 9437188
  0.0 4.2 %copy-start.2 = (s32[64]{0:T(128)S(1)}, s32[64]{0:T(128)}, u32[]{:S(2)}) copy-start(s32[64]{0:T(128)} %param.3) | copy-start | bytes 772
  2.8 6.5 %collective-permute-start = (bf16[256,3072]{1,0:T(8,128)(2,1)}, bf16[256,3072]{1,0:T(8,128)(2,1)}, u32[]{:S(2)}, u32[]{:S(2)}) collective-permute-start(bf16[256,3072]{1,0:T(8,128)(2,1)} %slice.21), channel_id=1, source_target_pairs={{4,0},{8,4},{12,8},{16,12},{20,16},{24,20},{28,24},{5,1},{9,5},{13... | collective-permute-start | bytes 4718600 | tf_op jit(solution)/shard_map/ppermute | solution.py:14
  12.3 2.2 %copy-start.1 = (bf16[1,64,2,3072]{3,2,1,0:T(2,128)(2,1)S(1)}, bf16[1,64,2,3072]{3,2,1,0:T(2,128)(2,1)}, u32[]{:S(2)}) copy-start(bf16[1,64,2,3072]{3,2,1,0:T(2,128)(2,1)} %stack.25) | copy-start | bytes 2359300
where the time goes:
time: 97 us; the launch traced here: 96.8 us
  blocking collectives  76.4 us (79%)
  local copies, waits for them, and re-layouts  11.2 us (12%)
  matrix products  4.92 us (5%)
  other arithmetic  2.86 us (3%)
  starting transfers between devices  1.28 us (1%)
    all_to_all x1, blocking collectives, local(): lax.all_to_all(owned, 'tm', split_axis=1, concat_axis=0, tiled=True)  58 us
    psum x1, blocking collectives, local(): return lax.psum(resident_gram_matrix, 'space')  18.4 us
    another operation x2, local copies, waits for them, and re-layouts, local(): owned = jnp.stack(pieces, axis=0).astype(jnp.bfloat16)  5.07 us
    dot_general x2, matrix products, local(): result = jnp.dot(table, segment, preferred_element_type=jnp.float32)  4.38 us
    slice x1, local copies, waits for them, and re-layouts, local(): leading = shifted(snapshots[:hop_len], 'tm', -1)  2.83 us
    all_to_all x2, local copies, waits for them, and re-layouts, local(): lax.all_to_all(owned, 'tm', split_axis=1, concat_axis=0, tiled=True)  2.33 us
    another operation x1, other arithmetic, local(): owned = jnp.stack(pieces, axis=0).astype(jnp.bfloat16)  2.07 us
  transfers between devices with their start and end apart: 1, of which 0 were waited for; matrix products, arithmetic and copies ran while one was open for 5% of the time, Pallas kernels for 0%

commit v1 on v0

--- a/solution.py
+++ b/solution.py
@@ -6,6 +6,12 @@
 
 NFFT = 512
 F = 64
+
+
+def gather_and_add(x, axis):
+    parts = lax.all_gather(x, axis, axis=0, tiled=False)
+    total = parts.sum(axis=0)
+    return total
 
 
 def shifted(block, axis, distance):
@@ -64,7 +70,7 @@
     resident_gram_matrix = (
         jnp.stack([gram_real_matrix, imag_gram], axis=1)[:, :, :blocks, :blocks] * scale
     )
-    return lax.psum(resident_gram_matrix, "space")
+    return gather_and_add(resident_gram_matrix, "space")
 
 
 def solution(mesh):

time: 97 us -> 88.7 us (0.914)
  blocking collectives: 76.4 us -> 68.1 us
    psum x1 -> x0, blocking collectives: 18.4 us -> none  [local(): return lax.psum(resident_gram_matrix, 'space')]
    all_gather x0 -> x1, blocking collectives: none -> 10 us  [gather_and_add(): parts = lax.all_gather(x, axis, axis=0, tiled=False)]
  transfers between devices with their start and end apart: 1 -> 1, of which waited for: 0 -> 0; matrix products, arithmetic and copies ran while one was open for 5% -> 6% of each run, Pallas kernels for 0% -> 0%
where the time goes in v1:
time: 88.7 us; the launch traced here: 88.5 us
  blocking collectives  68.1 us (77%)
  local copies, waits for them, and re-layouts  11.2 us (13%)
  matrix products  4.92 us (6%)
  other arithmetic  2.91 us (3%)
  starting transfers between devices  1.28 us (1%)
    all_to_all x1, blocking collectives, local(): lax.all_to_all(owned, 'tm', split_axis=1, concat_axis=0, tiled=True)  58 us
    all_gather x1, blocking collectives, gather_and_add(): parts = lax.all_gather(x, axis, axis=0, tiled=False)  10 us
    another operation x2, local copies, waits for them, and re-layouts, local(): owned = jnp.stack(pieces, axis=0).astype(jnp.bfloat16)  5.07 us
    dot_general x2, matrix products, local(): result = jnp.dot(table, segment, preferred_element_type=jnp.float32)  4.38 us
    slice x1, local copies, waits for them, and re-layouts, local(): leading = shifted(snapshots[:hop_len], 'tm', -1)  2.83 us
    all_to_all x2, local copies, waits for them, and re-layouts, local(): lax.all_to_all(owned, 'tm', split_axis=1, concat_axis=0, tiled=True)  2.33 us
    another operation x1, other arithmetic, local(): owned = jnp.stack(pieces, axis=0).astype(jnp.bfloat16)  2.07 us
  transfers between devices with their start and end apart: 1, of which 0 were waited for; matrix products, arithmetic and copies ran while one was open for 6% of the time, Pallas kernels for 0%

profile of v1, /device:TPU:0, one launch (start us, length us, event | category | flops | bytes accessed | tf_op | source)
XLA Modules:
  0.0 88.5 jit_solution(4166234434622462124)
XLA Ops:
  0.0 0.0 copy-start
  0.0 0.0 copy-start.2
  0.0 2.8 %slice.21 = bf16[256,3072]{1,0:T(8,128)(2,1)} slice(bf16[512,3072]{1,0:T(8,128)(2,1)} %param.2), slice={[0:256], [0:3072]} | slice | bytes 3145728 | tf_op jit(solution)/shard_map/slice | solution.py:39
  2.8 1.3 %collective-permute-start = (bf16[256,3072]{1,0:T(8,128)(2,1)}, bf16[256,3072]{1,0:T(8,128)(2,1)}, u32[]{:S(2)}, u32[]{:S(2)}) collective-permute-start(bf16[256,3072]{1,0:T(8,128)(2,1)} %slice.21), channel_id=1, source_target_pairs={{4,0},{8,4},{12,8},{16,12},{20,16},{24,20},{28,24},{5,1},{9,5},{13... | collective-permute-start | bytes 4718600 | tf_op jit(solution)/shard_map/ppermute | solution.py:20
  4.2 0.0 copy-done.2
  4.2 0.6 multiply_convert_fusion.1
  4.8 0.1 copy.12
  5.0 0.1 convert_element_type.35
  5.0 0.0 copy-done
  5.0 1.5 %fusion = bf16[128,3072]{1,0:T(8,128)(2,1)} fusion(bf16[128,512]{1,0:T(8,128)(2,1)S(1)} %convert_element_type.35, bf16[512,3072]{1,0:T(8,128)(2,1)S(1)} %copy-done, pred[]{:T(512)S(6)} %lt.12), kind=kOutput, calls=%fused_computation.2 | convolution fusion | flops 403439616 | bytes 4063233 | tf_op jit(solution)/shard_map/dot_general | solution.py:45
  6.5 2.8 %stack.25 = bf16[1,64,2,3072]{3,2,1,0:T(2,128)(2,1)} reshape(bf16[128,3072]{1,0:T(8,128)(2,1)} %fusion) | data formatting | bytes 1572864 | tf_op jit(solution)/shard_map/stack | solution.py:47
  9.4 0.0 collective-permute-done
  9.4 2.9 %fusion.1 = bf16[128,3072]{1,0:T(8,128)(2,1)} fusion(bf16[128,512]{1,0:T(8,128)(2,1)S(1)} %convert_element_type.35, bf16[256,3072]{1,0:T(8,128)(2,1)} %collective-permute-done, bf16[512,3072]{1,0:T(8,128)(2,1)S(1)} %copy-done, pred[]{:T(512)S(6)} %lt.14), kind=kOutput, calls=%fused_computation.3 | convolution fusion | flops 409731072 | bytes 5636097 | tf_op jit(solution)/shard_map/dot_general | solution.py:45
  12.3 0.0 copy-start.1
  12.3 2.2 %stack.26 = bf16[1,64,2,3072]{3,2,1,0:T(2,128)(2,1)S(1)} reshape(bf16[128,3072]{1,0:T(8,128)(2,1)} %fusion.1) | data formatting | bytes 1572864 | tf_op jit(solution)/shard_map/stack | solution.py:47
  14.5 0.0 copy-done.1
  14.5 2.1 %pad_maximum_fusion.2 = bf16[2,64,2,3072]{3,2,0,1:T(2,128)(2,1)S(1)} fusion(bf16[1,64,2,3072]{3,2,0,1:T(2,128)(2,1)S(1)} %bitcast.23, bf16[1,64,2,3072]{3,2,0,1:T(2,128)(2,1)S(1)} %bitcast.22), kind=kLoop, calls=%fused_computation.6 | loop fusion | flops 786432 | bytes 3145728 | tf_op jit(solution)/shard_map/stack | solution.py:47
  16.6 58.0 %all_to_all.18 = bf16[2,64,2,3072]{3,2,0,1:T(2,128)(2,1)S(1)} all-to-all(bf16[2,64,2,3072]{3,2,0,1:T(2,128)(2,1)S(1)} %pad_maximum_fusion.2), channel_id=1, replica_groups=mesh['tm'=8,'space'=4] {'tm'}, dimensions={1} | all-to-all | bytes 3145728 | tf_op jit(solution)/shard_map/all_to_all | solution.py:49
  74.6 1.7 %copy.15 = bf16[8,2,8,2,3072]{4,1,0,3,2:T(2,128)(2,1)S(1)} copy(bf16[8,2,8,2,3072]{4,3,1,2,0:T(2,128)(2,1)S(1)} %bitcast.21) | data formatting | bytes 3145728 | tf_op jit(solution)/shard_map/all_to_all | solution.py:49
  76.3 0.6 all_to_all.16
  76.9 0.5 fusion.14
  77.5 0.1 fusion.11
  77.6 10.0 %all-gather = f32[32,2,15,15]{3,2,0,1:T(8,128)S(1)} all-gather(f32[8,2,15,15]{3,2,0,1:T(8,128)S(1)} %fusion.6), channel_id=2, replica_groups=mesh['tm'=8,'space'=4] {'space'}, dimensions={0}, use_global_device_ids=true | all-gather | bytes 72000 | tf_op jit(solution)/shard_map/all_gather | solution.py:12
  87.7 0.1 reduce_sum.9
  87.7 0.7 copy.16
  (3 shorter events, 0.1 us)
Async XLA Ops:
  0.0 5.0 %copy-start = (bf16[512,3072]{1,0:T(8,128)(2,1)S(1)}, bf16[512,3072]{1,0:T(8,128)(2,1)}, u32[]{:S(2)}) copy-start(bf16[512,3072]{1,0:T(8,128)(2,1)} %param.2) | copy-start | bytes 9437188
  0.0 4.2 %copy-start.2 = (s32[64]{0:T(128)S(1)}, s32[64]{0:T(128)}, u32[]{:S(2)}) copy-start(s32[64]{0:T(128)} %param.3) | copy-start | bytes 772
  2.8 6.5 %collective-permute-start = (bf16[256,3072]{1,0:T(8,128)(2,1)}, bf16[256,3072]{1,0:T(8,128)(2,1)}, u32[]{:S(2)}, u32[]{:S(2)}) collective-permute-start(bf16[256,3072]{1,0:T(8,128)(2,1)} %slice.21), channel_id=1, source_target_pairs={{4,0},{8,4},{12,8},{16,12},{20,16},{24,20},{28,24},{5,1},{9,5},{13... | collective-permute-start | bytes 4718600 | tf_op jit(solution)/shard_map/ppermute | solution.py:20
  12.3 2.2 %copy-start.1 = (bf16[1,64,2,3072]{3,2,1,0:T(2,128)(2,1)S(1)}, bf16[1,64,2,3072]{3,2,1,0:T(2,128)(2,1)}, u32[]{:S(2)}) copy-start(bf16[1,64,2,3072]{3,2,1,0:T(2,128)(2,1)} %stack.25) | copy-start | bytes 2359300
